TPU v7x, 32 devices: a whole 2x2x4 slice. The times are simulated.
32 devices in a mesh: wide: 8 (over y, x, core), blk: 4 (over z).
Axes of the slice: x: 2, y: 2, z: 4, core: 2. Of those that a mesh axis runs over, the one named last changes fastest.
Arguments:
- audio: bfloat16 [4096, 1024], P(('wide', 'blk')), may hold values from -1 to 1
- video: bfloat16 [4096, 1024], P(('wide', 'blk')), may hold values from -1 to 1
- owner: int32 [4096, 1], P(('wide', 'blk')), may hold values from 0 to 7; in each aligned block of 128 rows (0 to 127, 128 to 255, ...) at most 32 rows name the same one
- clip_feats: bfloat16 [8192, 1024], P(('wide', 'blk')), may hold values from -24 to 24
- lengths: int32 [8192], P(('wide', 'blk')), may hold values from 1 to 16
- proj_weight: bfloat16 [1024, 1024], replicated, may hold values from -0.1875 to 0.1875
Outputs:
- audio_grad: bfloat16 [4096, 1024], P(('wide', 'blk'))
- feats_grad: bfloat16 [8192, 1024], P(('wide', 'blk'))
- weight_grad: float32 [1024, 1024], P('wide')
Inputs may be any that keep to these rules, and one draw needn't show every extreme that they name: Among the 128 rows of one device, no owner is named more than 32 times, a bound that some block reaches.
All inputs are finite; a program needn't handle non-finite values.
Results may differ from a plain program's by a relative error of at most 0.02.
Values may be sent and summed in bfloat16 or wider, within the bound.
A program may use at most 64 MiB of HBM per device.

v0:
```python
from functools import partial
import jax
import jax.numpy as jnp
from jax import lax
from jax.sharding import PartitionSpec as P


def rows_dot(matrix_a, matrix_b):
    return lax.dot_general(
        matrix_a, matrix_b, (((1,), (1,)), ((), ())), preferred_element_type=jnp.float32
    )


def cols_dot(matrix_a, matrix_b):
    return lax.dot_general(
        matrix_a, matrix_b, (((0,), (0,)), ((), ())), preferred_element_type=jnp.float32
    )


def pair_coeffs(scores, labels, factor):
    return (factor * (jax.nn.sigmoid(4.0 * scores - 2.0) - labels)).astype(jnp.bfloat16)


def shards(audio, video, owner, clip_feats, lengths, proj_weight):
    blocks = lax.axis_size("blk")
    clip_count = audio.shape[0]
    feature_count = audio.shape[1]
    factor = 4.0 / blocks
    row_ids = jnp.arange(clip_count, dtype=jnp.int32)
    offset = lax.axis_index("blk") * clip_count
    gathered = lax.all_gather(video, "blk", axis=0, tiled=True)
    other_ids = jnp.arange(gathered.shape[0], dtype=jnp.int32)
    labels = ((offset + row_ids)[:, None] == other_ids[None, :]).astype(jnp.float32)
    coeffs = pair_coeffs(rows_dot(audio, gathered), labels, factor)
    audio_total = jnp.dot(coeffs, gathered, preferred_element_type=jnp.float32)
    gathered = lax.all_gather(audio, "blk", axis=0, tiled=True)
    other_ids = jnp.arange(gathered.shape[0], dtype=jnp.int32)
    labels = (other_ids[:, None] == (offset + row_ids)[None, :]).astype(jnp.float32)
    coeffs = pair_coeffs(rows_dot(gathered, video), labels, factor)
    video_sum = cols_dot(coeffs, gathered)
    audio_grad = audio_total.astype(jnp.bfloat16)
    video_grad = video_sum.astype(jnp.bfloat16)
    peer_count = lax.axis_size("wide")
    slot_count = clip_feats.shape[0]
    capacity = slot_count // peer_count
    owner_peer = owner[:, 0]
    onehot = (owner_peer[:, None] == jnp.arange(peer_count, dtype=jnp.int32)[None, :]).astype(
        jnp.int32
    )
    slot_rank = jnp.sum((jnp.cumsum(onehot, axis=0) - onehot) * onehot, axis=1)
    target = owner_peer * capacity + slot_rank
    placing = (jnp.arange(slot_count, dtype=jnp.int32)[:, None] == target[None, :]).astype(
        jnp.bfloat16
    )
    packed = jnp.dot(placing, video_grad, preferred_element_type=jnp.float32).astype(jnp.bfloat16)
    packed = packed.reshape(peer_count, capacity, feature_count)
    received = lax.all_to_all(packed, "wide", split_axis=0, concat_axis=0, tiled=True).reshape(
        slot_count, feature_count
    )
    length_scale = lax.rsqrt(lengths.astype(jnp.float32))[:, None]
    pooled = (clip_feats.astype(jnp.float32) * length_scale).astype(jnp.bfloat16)
    preact = jnp.dot(pooled, proj_weight, preferred_element_type=jnp.float32)
    _, pullback = jax.vjp(partial(jax.nn.gelu, approximate=False), preact)
    pre_grad = pullback(received.astype(jnp.float32))[0].astype(jnp.bfloat16)
    feats_grad = (rows_dot(pre_grad, proj_weight) * length_scale).astype(jnp.bfloat16)
    partial_rows = lax.psum_scatter(
        cols_dot(pooled, pre_grad).astype(jnp.bfloat16), "wide", scatter_dimension=0, tiled=True
    )
    weight_grad = lax.psum(partial_rows, "blk").astype(jnp.float32)
    return (audio_grad, feats_grad, weight_grad)


def solution(mesh):
    return jax.shard_map(
        shards,
        mesh=mesh,
        in_specs=(
            P(("wide", "blk"), None),
            P(("wide", "blk"), None),
            P(("wide", "blk"), None),
            P(("wide", "blk"), None),
            P(("wide", "blk")),
            P(),
        ),
        out_specs=(P(("wide", "blk"), None), P(("wide", "blk"), None), P("wide", None)),
        check_vma=False,
    )
```

profile of v0, /device:TPU:0, one launch (start us, length us, event | category | flops | bytes accessed | tf_op | source)
XLA Modules:
  0.0 167.4 jit_solution(1915806834253951210)
XLA Ops:
  7.2 0.0 all-gather.5.cloned.1.call-start
  7.2 0.7 all-gather.5.cloned.1.call-update
  7.9 0.7 fusion.37
  8.7 0.2 reduce_window_sum.11
  8.8 0.8 select_reduce_fusion
  9.7 0.7 multiply_add_fusion
  10.3 30.0 %all-gather.5.cloned.1.call-done = bf16[512,1024]{1,0:T(8,128)(2,1)} async-done(((bf16[128,1024]{1,0:T(8,128)(2,1)}), bf16[512,1024]{1,0:T(8,128)(2,1)}) %all-gather.5.cloned.1.call-update) | async-done | bytes 1048592 | tf_op jit(solution)/shard_map/all_gather | solution.py:36
  40.3 1.8 %fusion.14 = bf16[512,128]{1,0:T(8,128)(2,1)S(1)} fusion(bf16[512,1024]{1,0:T(8,128)(2,1)} %all-gather.5.cloned.1.call-done, bf16[128,1024]{1,0:T(8,128)(2,1)} %param.7, s32[128]{0:T(128)S(1)} %iota_add_fusion), kind=kOutput, calls=%fused_computation.24 | convolution fusion | flops 134807552 | bytes 1442304 | tf_op jit(solution)/shard_map/dot_general | solution.py:9
  42.1 1.4 convolution_convert_fusion.1
  43.5 3.7 %all-to-all-start = ((bf16[8,32,1024]{2,1,0:T(8,128)(2,1)}), bf16[8,32,1024]{2,1,0:T(8,128)(2,1)S(1)}, u32[]{:S(2)}, u32[]{:S(2)}) async-start(bf16[8,32,1024]{2,1,0:T(8,128)(2,1)} %bitcast.1), calls=%async_computation | async-start | bytes 1048576 | tf_op jit(solution)/shard_map/all_to_all | solution.py:57
  47.2 0.0 all-gather.3.cloned.1.call-start
  47.2 0.7 all-gather.3.cloned.1.call-update
  47.9 0.0 reduce-scatter.2.cloned.1.call-start
  48.0 8.9 %all-to-all-done = bf16[8,32,1024]{2,1,0:T(8,128)(2,1)S(1)} async-done(((bf16[8,32,1024]{2,1,0:T(8,128)(2,1)}), bf16[8,32,1024]{2,1,0:T(8,128)(2,1)S(1)}, u32[]{:S(2)}, u32[]{:S(2)}) %all-to-all-start) | async-done | bytes 524320 | tf_op jit(solution)/shard_map/all_to_all | solution.py:57
  56.9 4.2 %fusion.20 = bf16[256,1024]{1,0:T(8,128)(2,1)S(1)} fusion(bf16[8,32,1024]{2,1,0:T(8,128)(2,1)S(1)} %all-to-all-done, bf16[1024,1024]{1,0:T(8,128)(2,1)S(1)} %copy-done, bf16[256,1024]{1,0:T(8,128)(2,1)} %param.9, f32[256]{0:T(256)S(1)} %convert_rsqrt_fusion), kind=kOutput, calls=%fused_computation.30 | convolution fusion | flops 556793856 | bytes 3671040 | tf_op jit(solution)/shard_map/dot_general | solution.py:62
  61.1 0.8 copy-done.3
  61.9 2.2 %convolution_convert_fusion = bf16[1024,1024]{1,0:T(8,128)(2,1)} fusion(bf16[256,1024]{1,0:T(8,128)(2,1)S(1)} %fusion.20, bf16[256,1024]{1,0:T(8,128)(2,1)S(1)} %copy-done.2, f32[256]{0:T(256)S(1)} %convert_rsqrt_fusion), kind=kOutput, calls=%fused_computation | convolution fusion | flops 538705920 | bytes 3146752 | tf_op jit(solution)/shard_map/dot_general | solution.py:15
  64.1 0.0 all-reduce.2.cloned.1.call-start
  64.2 13.3 %all-gather.3.cloned.1.call-done = bf16[512,1024]{1,0:T(8,128)(2,1)} async-done(((bf16[128,1024]{1,0:T(8,128)(2,1)}), bf16[512,1024]{1,0:T(8,128)(2,1)}) %all-gather.3.cloned.1.call-update) | async-done | bytes 1048592 | tf_op jit(solution)/shard_map/all_gather | solution.py:31
  77.5 3.1 %convolution_convert_fusion.3 = bf16[128,1024]{1,0:T(8,128)(2,1)} fusion(bf16[512,1024]{1,0:T(8,128)(2,1)} %all-gather.3.cloned.1.call-done, bf16[128,1024]{1,0:T(8,128)(2,1)S(1)} %copy-done.5, s32[128]{0:T(128)S(1)} %iota_add_fusion), kind=kOutput, calls=%fused_computation.8 | convolution fusion | flops 269156352 | bytes 1573376 | tf_op jit(solution)/shard_map/dot_general | solution.py:35
  80.5 40.8 %reduce-scatter.2.cloned.1.call-done = bf16[128,1024]{1,0:T(8,128)(2,1)} async-done(((bf16[1024,1024]{1,0:T(8,128)(2,1)}), bf16[128,1024]{1,0:T(8,128)(2,1)}) %reduce-scatter.2.cloned.1.call-update) | async-done | bytes 262160 | tf_op jit(solution)/shard_map/reduce_scatter | solution.py:66
  121.3 1.6 fusion
  122.9 36.2 %all-reduce.2.cloned.1.call-done = bf16[128,1024]{1,0:T(8,128)(2,1)} async-done(((bf16[128,1024]{1,0:T(8,128)(2,1)}), bf16[128,1024]{1,0:T(8,128)(2,1)}) %all-reduce.2.cloned.1.call-update) | async-done | bytes 262160 | tf_op jit(solution)/shard_map/psum | solution.py:69
  159.1 1.8 %convert_element_type.68 = f32[128,1024]{1,0:T(8,128)} convert(bf16[128,1024]{1,0:T(8,128)(2,1)} %all-reduce.2.cloned.1.call-done) | non-fusion elementwise | flops 131072 | bytes 786432 | tf_op jit(solution)/shard_map/convert_element_type | solution.py:69
  (17 shorter events, 0.1 us)
Async XLA Ops:
  7.2 49.7 %copy-start = (bf16[1024,1024]{1,0:T(8,128)(2,1)S(1)}, bf16[1024,1024]{1,0:T(8,128)(2,1)}, u32[]{:S(2)}) copy-start(bf16[1024,1024]{1,0:T(8,128)(2,1)} %param.11) | copy-start | bytes 6291460
  7.2 33.1 %all-gather.5.cloned.1.call-start = ((), (), s32[]{:S(2)}) async-start(), calls=%async_computation.3 | async-start | bytes 1310720 | tf_op jit(solution)/shard_map/all_gather | solution.py:36
  40.3 1.8 %copy-start.1 = (bf16[512,1024]{1,0:T(8,128)(2,1)S(1)}, bf16[512,1024]{1,0:T(8,128)(2,1)}, u32[]{:S(2)}) copy-start(bf16[512,1024]{1,0:T(8,128)(2,1)} %all-gather.5.cloned.1.call-done) | copy-start | bytes 3145732
  42.1 5.8 %copy-start.6 = (s32[256]{0:T(256)S(1)}, s32[256]{0:T(256)}, u32[]{:S(2)}) copy-start(s32[256]{0:T(256)} %param.10) | copy-start | bytes 3076
  43.5 13.4 %all-to-all-start = ((bf16[8,32,1024]{2,1,0:T(8,128)(2,1)}), bf16[8,32,1024]{2,1,0:T(8,128)(2,1)S(1)}, u32[]{:S(2)}, u32[]{:S(2)}) async-start(bf16[8,32,1024]{2,1,0:T(8,128)(2,1)} %bitcast.1), calls=%async_computation | async-start | bytes 1048576 | tf_op jit(solution)/shard_map/all_to_all | solution.py:57
  47.2 30.3 %all-gather.3.cloned.1.call-start = ((), (), s32[]{:S(2)}) async-start(), calls=%async_computation.2 | async-start | bytes 1310720 | tf_op jit(solution)/shard_map/all_gather | solution.py:31
  47.9 73.4 %reduce-scatter.2.cloned.1.call-start = ((), (), s32[]{:S(2)}) async-start(), calls=%async_computation.4 | async-start | bytes 2359296 | tf_op jit(solution)/shard_map/reduce_scatter | solution.py:66
  48.0 13.9 %copy-start.2 = (bf16[256,1024]{1,0:T(8,128)(2,1)S(1)}, bf16[256,1024]{1,0:T(8,128)(2,1)}, u32[]{:S(2)}) copy-start(bf16[256,1024]{1,0:T(8,128)(2,1)} %param.9) | copy-start | bytes 1572868
  61.1 0.8 copy-start.3
  61.9 15.6 %copy-start.5 = (bf16[128,1024]{1,0:T(8,128)(2,1)S(1)}, bf16[128,1024]{1,0:T(8,128)(2,1)}, u32[]{:S(2)}) copy-start(bf16[128,1024]{1,0:T(8,128)(2,1)} %param.6) | copy-start | bytes 786436
  64.1 57.2 %copy-start.4 = (bf16[256,1024]{1,0:T(8,128)(2,1)S(1)}, bf16[256,1024]{1,0:T(8,128)(2,1)}, u32[]{:S(2)}) copy-start(bf16[256,1024]{1,0:T(8,128)(2,1)} %copy-done.3) | copy-start | bytes 1572868
  64.1 95.0 %all-reduce.2.cloned.1.call-start = ((), (), s32[]{:S(2)}) async-start(), calls=%async_computation.5 | async-start | bytes 524288 | tf_op jit(solution)/shard_map/psum | solution.py:69
Sparse Core Ops, SparseCore 0:
  9.6 30.6 all-gather.4
  49.5 27.8 all-gather.2
  80.7 40.4 reduce-scatter.1
  123.5 35.5 all-reduce.1
where the time goes:
time: 168 us; the launch traced here: 167 us
  waiting for transfers between devices  131 us (78%)
  matrix products  14.2 us (8%)
  between operations  13.9 us (8%)
  other arithmetic  4.2 us (2%)
  starting transfers between devices  3.81 us (2%)
    reduce_scatter x1, waiting for transfers between devices, shards(): lax.psum_scatter(cols_dot(pooled, pre_grad).astype(jnp.bfloat16), 'wide',...  40.8 us
    psum x1, waiting for transfers between devices, shards(): weight_grad = lax.psum(partial_rows, 'blk').astype(jnp.float32)  36.2 us
    all_gather x1, waiting for transfers between devices, shards(): gathered = lax.all_gather(audio, 'blk', axis=0, tiled=True)  30 us
    all_gather x1, waiting for transfers between devices, shards(): gathered = lax.all_gather(video, 'blk', axis=0, tiled=True)  13.3 us
    all_to_all x1, waiting for transfers between devices, shards(): lax.all_to_all(packed, 'wide', split_axis=0, concat_axis=0, tiled=True)  8.88 us
    dot_general x1, matrix products, shards(): preact = jnp.dot(pooled, proj_weight, preferred_element_type=jnp.float32)  4.22 us
    all_to_all x1, starting transfers between devices, shards(): lax.all_to_all(packed, 'wide', split_axis=0, concat_axis=0, tiled=True)  3.65 us
    dot_general x2, matrix products, rows_dot(): lax.dot_general(matrix_a, matrix_b, (((1,), (1,)), ((), ())), preferred_e...  3.41 us
  transfers between devices with their start and end apart: 5, of which 5 were waited for; matrix products, arithmetic and copies ran while one was open for 8% of the time, Pallas kernels for 0%

commit v1 on v0

--- a/solution.py
+++ b/solution.py
@@ -33,7 +33,10 @@
     labels = ((offset + row_ids)[:, None] == other_ids[None, :]).astype(jnp.float32)
     coeffs = pair_coeffs(rows_dot(audio, gathered), labels, factor)
     audio_total = jnp.dot(coeffs, gathered, preferred_element_type=jnp.float32)
-    gathered = lax.all_gather(audio, "blk", axis=0, tiled=True)
+    count = lax.axis_size("blk")
+    pieces = jnp.stack([audio for _ in range(count)])
+    pieces = lax.all_to_all(pieces, "blk", split_axis=0, concat_axis=0)
+    gathered = jnp.concatenate(pieces, axis=0)
     other_ids = jnp.arange(gathered.shape[0], dtype=jnp.int32)
     labels = (other_ids[:, None] == (offset + row_ids)[None, :]).astype(jnp.float32)
     coeffs = pair_coeffs(rows_dot(gathered, video), labels, factor)

time: 168 us -> 149 us (0.89)
  waiting for transfers between devices: 131 us -> 104 us
  starting transfers between devices: 3.81 us -> 10.2 us
  local copies, waits for them, and re-layouts: 0.82 us -> 3.02 us
  other arithmetic: 4.2 us -> 2.23 us
  between operations: 13.9 us -> 15.6 us
    all_gather x1 -> x0, waiting for transfers between devices: 30 us -> none  [shards(): gathered = lax.all_gather(audio, 'blk', axis=0, tiled=True)]
    all_to_all x0 -> x1, waiting for transfers between devices: none -> 25.3 us  [shards(): pieces = lax.all_to_all(pieces, 'blk', split_axis=0, concat_axis=0)]
    reduce_scatter x1, waiting for transfers between devices: 40.8 us -> 22.3 us  [shards(): lax.psum_scatter(cols_dot(pooled, pre_grad).astype(jnp.bfloat16), 'wide',...]
    all_to_all x0 -> x1, starting transfers between devices: none -> 6.35 us  [shards(): pieces = lax.all_to_all(pieces, 'blk', split_axis=0, concat_axis=0)]
    another operation x0 -> x1, local copies, waits for them, and re-layouts: none -> 2.19 us  [shards(): pieces = jnp.stack([audio for _ in range(count)])]
    psum x1, waiting for transfers between devices: 36.2 us -> 34.2 us  [shards(): weight_grad = lax.psum(partial_rows, 'blk').astype(jnp.float32)]
where the time goes in v1:
time: 149 us; the launch traced here: 148 us
  waiting for transfers between devices  104 us (70%)
  between operations  15.6 us (10%)
  matrix products  12.8 us (9%)
  starting transfers between devices  10.2 us (7%)
  local copies, waits for them, and re-layouts  3.02 us (2%)
  other arithmetic  2.23 us (1%)
    psum x1, waiting for transfers between devices, shards(): weight_grad = lax.psum(partial_rows, 'blk').astype(jnp.float32)  34.2 us
    all_to_all x1, waiting for transfers between devices, shards(): pieces = lax.all_to_all(pieces, 'blk', split_axis=0, concat_axis=0)  25.3 us
    reduce_scatter x1, waiting for transfers between devices, shards(): lax.psum_scatter(cols_dot(pooled, pre_grad).astype(jnp.bfloat16), 'wide',...  22.3 us
    all_gather x1, waiting for transfers between devices, shards(): gathered = lax.all_gather(video, 'blk', axis=0, tiled=True)  13 us
    all_to_all x1, waiting for transfers between devices, shards(): lax.all_to_all(packed, 'wide', split_axis=0, concat_axis=0, tiled=True)  8.89 us
    all_to_all x1, starting transfers between devices, shards(): pieces = lax.all_to_all(pieces, 'blk', split_axis=0, concat_axis=0)  6.35 us
    dot_general x1, matrix products, shards(): preact = jnp.dot(pooled, proj_weight, preferred_element_type=jnp.float32)  4.22 us
    all_to_all x1, starting transfers between devices, shards(): lax.all_to_all(packed, 'wide', split_axis=0, concat_axis=0, tiled=True)  3.72 us
  transfers between devices with their start and end apart: 5, of which 5 were waited for; matrix products, arithmetic and copies ran while one was open for 8% of the time, Pallas kernels for 0%

profile of v1, /device:TPU:0, one launch (start us, length us, event | category | flops | bytes accessed | tf_op | source)
XLA Modules:
  0.0 148.1 jit_solution(2604914790261383413)
XLA Ops:
  8.0 2.2 %stack.2 = bf16[4,128,1024]{2,1,0:T(8,128)(2,1)} broadcast(bf16[128,1024]{1,0:T(8,128)(2,1)} %param.6), dimensions={1,2} | broadcast | bytes 1310720 | tf_op jit(solution)/shard_map/stack | solution.py:37
  10.2 6.3 %all-to-all-start = ((bf16[4,128,1024]{2,1,0:T(8,128)(2,1)}), bf16[4,128,1024]{2,1,0:T(8,128)(2,1)S(1)}, u32[]{:S(2)}, u32[]{:S(2)}) async-start(bf16[4,128,1024]{2,1,0:T(8,128)(2,1)} %stack.2), calls=%async_computation | async-start | bytes 2097152 | tf_op jit(solution)/shard_map/all_to_all | solution.py:38
  16.6 0.1 fusion.37
  16.7 0.2 reduce_window_sum.11
  16.8 0.2 select_reduce_fusion
  17.0 25.3 %all-to-all-done = bf16[4,128,1024]{2,1,0:T(8,128)(2,1)S(1)} async-done(((bf16[4,128,1024]{2,1,0:T(8,128)(2,1)}), bf16[4,128,1024]{2,1,0:T(8,128)(2,1)S(1)}, u32[]{:S(2)}, u32[]{:S(2)}) %all-to-all-start) | async-done | bytes 1048608 | tf_op jit(solution)/shard_map/all_to_all | solution.py:38
  42.3 0.5 fusion.14
  42.8 1.4 convolution_convert_fusion.1
  44.1 3.7 %all-to-all-start.1 = ((bf16[8,32,1024]{2,1,0:T(8,128)(2,1)}), bf16[8,32,1024]{2,1,0:T(8,128)(2,1)S(1)}, u32[]{:S(2)}, u32[]{:S(2)}) async-start(bf16[8,32,1024]{2,1,0:T(8,128)(2,1)} %bitcast.20), calls=%async_computation.1 | async-start | bytes 1048576 | tf_op jit(solution)/shard_map/all_to_all | solution.py:60
  47.9 0.0 all-gather.2.cloned.1.call-start
  47.9 0.7 all-gather.2.cloned.1.call-update
  48.6 0.0 reduce-scatter.2.cloned.1.call-start
  48.7 8.9 %all-to-all-done.1 = bf16[8,32,1024]{2,1,0:T(8,128)(2,1)S(1)} async-done(((bf16[8,32,1024]{2,1,0:T(8,128)(2,1)}), bf16[8,32,1024]{2,1,0:T(8,128)(2,1)S(1)}, u32[]{:S(2)}, u32[]{:S(2)}) %all-to-all-start.1) | async-done | bytes 524320 | tf_op jit(solution)/shard_map/all_to_all | solution.py:60
  57.6 4.2 %fusion.20 = bf16[256,1024]{1,0:T(8,128)(2,1)S(1)} fusion(bf16[8,32,1024]{2,1,0:T(8,128)(2,1)S(1)} %all-to-all-done.1, bf16[1024,1024]{1,0:T(8,128)(2,1)S(1)} %copy-done, bf16[256,1024]{1,0:T(8,128)(2,1)} %param.9, f32[256]{0:T(256)S(1)} %convert_rsqrt_fusion), kind=kOutput, calls=%fused_computation.30 | convolution fusion | flops 556793856 | bytes 3671040 | tf_op jit(solution)/shard_map/dot_general | solution.py:65
  61.8 0.8 copy-done.2
  62.6 2.2 %convolution_convert_fusion = bf16[1024,1024]{1,0:T(8,128)(2,1)} fusion(bf16[256,1024]{1,0:T(8,128)(2,1)S(1)} %fusion.20, bf16[256,1024]{1,0:T(8,128)(2,1)S(1)} %copy-done.1, f32[256]{0:T(256)S(1)} %convert_rsqrt_fusion), kind=kOutput, calls=%fused_computation | convolution fusion | flops 538705920 | bytes 3146752 | tf_op jit(solution)/shard_map/dot_general | solution.py:15
  64.8 0.0 reduce-scatter.2.cloned.1.call-update
  64.8 0.0 all-reduce.2.cloned.1.call-start
  64.9 13.0 %all-gather.2.cloned.1.call-done = bf16[512,1024]{1,0:T(8,128)(2,1)} async-done(((bf16[128,1024]{1,0:T(8,128)(2,1)}), bf16[512,1024]{1,0:T(8,128)(2,1)}) %all-gather.2.cloned.1.call-update) | async-done | bytes 1048592 | tf_op jit(solution)/shard_map/all_gather | solution.py:31
  77.8 3.0 %convolution_convert_fusion.3 = bf16[128,1024]{1,0:T(8,128)(2,1)} fusion(bf16[512,1024]{1,0:T(8,128)(2,1)} %all-gather.2.cloned.1.call-done, bf16[128,1024]{1,0:T(8,128)(2,1)S(1)} %copy-done.4, s32[128]{0:T(128)S(1)} %iota_add_fusion), kind=kOutput, calls=%fused_computation.8 | convolution fusion | flops 269156352 | bytes 1573376 | tf_op jit(solution)/shard_map/dot_general | solution.py:35
  80.9 22.3 %reduce-scatter.2.cloned.1.call-done = bf16[128,1024]{1,0:T(8,128)(2,1)} async-done(((bf16[1024,1024]{1,0:T(8,128)(2,1)}), bf16[128,1024]{1,0:T(8,128)(2,1)}) %reduce-scatter.2.cloned.1.call-update) | async-done | bytes 262160 | tf_op jit(solution)/shard_map/reduce_scatter | solution.py:69
  103.2 1.5 %fusion = bf16[256,1024]{1,0:T(8,128)(2,1)} fusion(bf16[256,1024]{1,0:T(8,128)(2,1)S(1)} %copy-done.3, bf16[1024,1024]{1,0:T(8,128)(2,1)S(1)} %copy-done, f32[256]{0:T(256)S(1)} %convert_rsqrt_fusion), kind=kOutput, calls=%fused_computation.5 | convolution fusion | flops 537395200 | bytes 3146752 | tf_op jit(solution)/shard_map/dot_general | solution.py:9
  104.7 34.2 %all-reduce.2.cloned.1.call-done = bf16[128,1024]{1,0:T(8,128)(2,1)} async-done(((bf16[128,1024]{1,0:T(8,128)(2,1)}), bf16[128,1024]{1,0:T(8,128)(2,1)}) %all-reduce.2.cloned.1.call-update) | async-done | bytes 262160 | tf_op jit(solution)/shard_map/psum | solution.py:72
  138.9 1.8 %convert_element_type.68 = f32[128,1024]{1,0:T(8,128)} convert(bf16[128,1024]{1,0:T(8,128)(2,1)} %all-reduce.2.cloned.1.call-done) | non-fusion elementwise | flops 131072 | bytes 786432 | tf_op jit(solution)/shard_map/convert_element_type | solution.py:72
  (19 shorter events, 0.1 us)
Async XLA Ops:
  8.0 49.6 %copy-start = (bf16[1024,1024]{1,0:T(8,128)(2,1)S(1)}, bf16[1024,1024]{1,0:T(8,128)(2,1)}, u32[]{:S(2)}) copy-start(bf16[1024,1024]{1,0:T(8,128)(2,1)} %param.11) | copy-start | bytes 6291460
  8.0 8.6 %copy-start.6 = (s32[128,1]{0,1:T(1,128)S(1)}, s32[128,1]{0,1:T(1,128)}, u32[]{:S(2)}) copy-start(s32[128,1]{0,1:T(1,128)} %param.8) | copy-start | bytes 1540
  8.0 34.3 %copy-start.5 = (bf16[128,1024]{1,0:T(8,128)(2,1)S(1)}, bf16[128,1024]{1,0:T(8,128)(2,1)}, u32[]{:S(2)}) copy-start(bf16[128,1024]{1,0:T(8,128)(2,1)} %param.7) | copy-start | bytes 786436
  10.2 32.1 %all-to-all-start = ((bf16[4,128,1024]{2,1,0:T(8,128)(2,1)}), bf16[4,128,1024]{2,1,0:T(8,128)(2,1)S(1)}, u32[]{:S(2)}, u32[]{:S(2)}) async-start(bf16[4,128,1024]{2,1,0:T(8,128)(2,1)} %stack.2), calls=%async_computation | async-start | bytes 2097152 | tf_op jit(solution)/shard_map/all_to_all | solution.py:38
  42.8 5.9 %copy-start.7 = (s32[256]{0:T(256)S(1)}, s32[256]{0:T(256)}, u32[]{:S(2)}) copy-start(s32[256]{0:T(256)} %param.10) | copy-start | bytes 3076
  44.1 13.4 %all-to-all-start.1 = ((bf16[8,32,1024]{2,1,0:T(8,128)(2,1)}), bf16[8,32,1024]{2,1,0:T(8,128)(2,1)S(1)}, u32[]{:S(2)}, u32[]{:S(2)}) async-start(bf16[8,32,1024]{2,1,0:T(8,128)(2,1)} %bitcast.20), calls=%async_computation.1 | async-start | bytes 1048576 | tf_op jit(solution)/shard_map/all_to_all | solution.py:60
  47.9 30.0 %all-gather.2.cloned.1.call-start = ((), (), s32[]{:S(2)}) async-start(), calls=%async_computation.3 | async-start | bytes 1310720 | tf_op jit(solution)/shard_map/all_gather | solution.py:31
  48.6 54.5 %reduce-scatter.2.cloned.1.call-start = ((), (), s32[]{:S(2)}) async-start(), calls=%async_computation.4 | async-start | bytes 2359296 | tf_op jit(solution)/shard_map/reduce_scatter | solution.py:69
  48.7 13.9 %copy-start.1 = (bf16[256,1024]{1,0:T(8,128)(2,1)S(1)}, bf16[256,1024]{1,0:T(8,128)(2,1)}, u32[]{:S(2)}) copy-start(bf16[256,1024]{1,0:T(8,128)(2,1)} %param.9) | copy-start | bytes 1572868
  61.8 0.8 copy-start.2
  62.6 15.2 %copy-start.4 = (bf16[128,1024]{1,0:T(8,128)(2,1)S(1)}, bf16[128,1024]{1,0:T(8,128)(2,1)}, u32[]{:S(2)}) copy-start(bf16[128,1024]{1,0:T(8,128)(2,1)} %param.6) | copy-start | bytes 786436
  64.8 38.4 %copy-start.3 = (bf16[256,1024]{1,0:T(8,128)(2,1)S(1)}, bf16[256,1024]{1,0:T(8,128)(2,1)}, u32[]{:S(2)}) copy-start(bf16[256,1024]{1,0:T(8,128)(2,1)} %copy-done.2) | copy-start | bytes 1572868
  64.8 74.0 %all-reduce.2.cloned.1.call-start = ((), (), s32[]{:S(2)}) async-start(), calls=%async_computation.5 | async-start | bytes 524288 | tf_op jit(solution)/shard_map/psum | solution.py:72
Sparse Core Ops, SparseCore 0:
  50.2 27.5 all-gather.1
  103.3 35.5 all-reduce.1
Sparse Core Ops, SparseCore 1:
  64.9 38.2 reduce-scatter.1
